TPU v7x, 128 devices: a whole 4x4x4 slice. The times are simulated.
128 devices in a mesh: gx: 16 (over z_lo, y, core), gy: 8 (over x, z_hi).
Axes of the slice: x: 4, y: 4, z: 4 (z_hi: 2, z_lo: 2; z = z_hi * 2 + z_lo), core: 2. Of those that a mesh axis runs over, the one named last changes fastest.
Arguments:
- field_e: float32 [3, 256, 128, 256], P(None, 'gx', 'gy'), may hold values from -6 to 6
- field_h: float32 [3, 256, 128, 256], P(None, 'gx', 'gy'), may hold values from -6 to 6
- density: float32 [2, 8, 8, 2097152], P(None, None, None, ('gx', 'gy')), may hold values from -1.8 to 1.8
- dipole: float32 [3, 2097152], P(None, ('gx', 'gy')), may hold values from -6 to 6
- levels: float32 [8], replicated, may hold values from -3 to 3
- coupling: float32 [8, 8], replicated, may hold values from -2 to 2
- rates: float32 [8, 8], replicated, may hold values from 0.1 to 3
- tile_cells: int32 [16384], P(('gx', 'gy')), may hold values from 0 to 511, as said below
- tile_owner: int32 [16384, 1], P(('gx', 'gy')), may hold values from 0 to 127; in each aligned block of 128 rows (0 to 127, 128 to 255, ...) at most 2 rows name the same one
- emitter_offsets: int32 [16384, 64], P(('gx', 'gy')), may hold values from 0 to 127
Outputs:
- electric_out: float32 [3, 256, 128, 256], P(None, 'gx', 'gy')
- magnetic_out: float32 [3, 256, 128, 256], P(None, 'gx', 'gy')
- density_out: float32 [2, 8, 8, 2097152], P(None, None, None, ('gx', 'gy'))
Inputs may be any that keep to these rules, and one draw needn't show every extreme that they name: `tile_cells`: within one device's 128 entries the local tile numbers are distinct. `tile_owner`: among the 128 tiles of one device no owner is named more than 2 times.
All inputs are finite; a program needn't handle non-finite values.
Results may differ from a plain program's by a relative error of at most 0.0003.
Values sent between devices are 32-bit elements; how exact they have to be, the bound alone decides.
A program may use at most 320 MiB of HBM per device.

v0:
```python
import jax
import jax.numpy as jnp
from jax import lax
from jax.sharding import PartitionSpec as P

TILE = 128
STEPS = 4
courant = 0.5
time_step = 0.12


def passed_along(block, axis, distance):
    devices = range(lax.axis_size(axis))
    route = [(i - distance, i) for i in devices if i - distance in devices]
    return lax.ppermute(block, axis, route)


def forward(values_in, beyond, along):
    length = values_in.shape[along]
    return (
        jnp.concatenate([lax.slice_in_dim(values_in, 1, length, axis=along), beyond], axis=along)
        - values_in
    )


def backward(values_in, behind_slab, along):
    length = values_in.shape[along]
    return values_in - jnp.concatenate(
        [behind_slab, lax.slice_in_dim(values_in, 0, length - 1, axis=along)], axis=along
    )


def zero_edge(values_in, along):
    return jnp.zeros_like(lax.slice_in_dim(values_in, 0, 1, axis=along))


def curl_ahead(fields, planes, rows):
    curl_one = forward(fields[2], rows[1], 1) - forward(fields[1], zero_edge(fields[1], 2), 2)
    curl_two = forward(fields[0], zero_edge(fields[0], 2), 2) - forward(fields[2], planes[1], 0)
    curl_three = forward(fields[1], planes[0], 0) - forward(fields[0], rows[0], 1)
    return jnp.stack([curl_one, curl_two, curl_three])


def curl_behind(fields, planes, rows):
    curl_one = backward(fields[2], rows[1], 1) - backward(fields[1], zero_edge(fields[1], 2), 2)
    curl_two = backward(fields[0], zero_edge(fields[0], 2), 2) - backward(fields[2], planes[1], 0)
    curl_three = backward(fields[1], planes[0], 0) - backward(fields[0], rows[0], 1)
    return jnp.stack([curl_one, curl_two, curl_three])


def commutator(symmetric, matrix):
    result = jnp.zeros_like(matrix)
    for inner in range(matrix.shape[0]):
        result = result + symmetric[:, inner][:, None, None] * matrix[inner][None, :, :]
        result = result - matrix[:, inner][:, None, :] * symmetric[inner][None, :, None]
    return result


def advance_driven(states, driving, levels, symmetric, damping):
    real_part = states[0]
    imag_part = states[1]
    spacing = (levels[:, None] - levels[None, :])[:, :, None]
    decays = damping[:, :, None]
    comm_imag = commutator(symmetric, imag_part)
    comm_real = commutator(symmetric, real_part)
    change_real = spacing * imag_part + driving * comm_imag - decays * real_part
    change_imag = -spacing * real_part - driving * comm_real - decays * imag_part
    moved = time_step * jnp.sum(symmetric[:, :, None] * change_real, axis=(0, 1))
    updated = jnp.stack([real_part + time_step * change_real, imag_part + time_step * change_imag])
    return (updated, moved)


def advance(states, orient, samples, levels, symmetric, damping):
    driving = orient[0] * samples[0] + orient[1] * samples[1] + orient[2] * samples[2]
    updated, moved = advance_driven(states, driving, levels, symmetric, damping)
    return (updated, moved[None, :] * orient)


def body(
    field_e,
    field_h,
    density,
    dipole,
    levels,
    coupling,
    rates,
    tile_cells,
    tile_owner,
    emitter_offsets,
):
    count_x = lax.axis_size("gx")
    count_y = lax.axis_size("gy")
    devices = count_x * count_y
    tile_count = tile_cells.shape[0]
    per_tile = emitter_offsets.shape[1]
    capacity = density.shape[3] // (devices * per_tile)
    symmetric = 0.5 * (coupling + coupling.T)
    damping = 0.5 * (rates + rates.T) * (1.0 - jnp.eye(coupling.shape[0], dtype=jnp.float32))
    positions = (tile_cells[:, None] * TILE + emitter_offsets).reshape(-1)
    owners = tile_owner[:, 0]
    ordinal = jnp.arange(tile_count, dtype=jnp.int32)
    earlier = ordinal[None, :] < ordinal[:, None]
    matches = owners[:, None] == owners[None, :]
    ranking = jnp.sum(jnp.where(matches & earlier, 1, 0), axis=1).astype(jnp.int32)
    slot_rows = owners * capacity + ranking
    for repeat in range(STEPS):
        ahead_planes = passed_along(field_e[1:3, 0:1], "gx", -1)
        ahead_rows = passed_along(field_e[0::2, :, 0:1], "gy", -1)
        field_h = field_h - courant * curl_ahead(field_e, ahead_planes, ahead_rows)
        behind_planes = passed_along(field_h[1:3, -1:], "gx", 1)
        behind_rows = passed_along(field_h[0::2, :, -1:], "gy", 1)
        field_e = field_e + courant * curl_behind(field_h, behind_planes, behind_rows)
        flattened = field_e.reshape(3, -1)
        samples = flattened[:, positions].reshape(3, tile_count, per_tile)
        outgoing = (
            jnp.zeros((3, devices * capacity, per_tile), jnp.float32)
            .at[:, slot_rows, :]
            .set(samples)
        )
        incoming = lax.all_to_all(
            outgoing.reshape(3, devices, -1), ("gx", "gy"), split_axis=1, concat_axis=1, tiled=True
        )
        density, feed_terms = advance(
            density, dipole, incoming.reshape(3, -1), levels, symmetric, damping
        )
        returned = lax.all_to_all(
            feed_terms.reshape(3, devices, -1),
            ("gx", "gy"),
            split_axis=1,
            concat_axis=1,
            tiled=True,
        )
        back_terms = returned.reshape(3, devices * capacity, per_tile)[:, slot_rows, :].reshape(
            3, -1
        )
        flattened = flattened.at[:, positions].add(-back_terms)
        field_e = flattened.reshape(field_e.shape)
    return (field_e, field_h, density)


def solution(mesh):
    placed = (
        P(None, "gx", "gy", None),
        P(None, "gx", "gy", None),
        P(None, None, None, ("gx", "gy")),
        P(None, ("gx", "gy")),
        P(),
        P(),
        P(),
        P(("gx", "gy")),
        P(("gx", "gy"), None),
        P(("gx", "gy"), None),
    )
    return jax.shard_map(
        body,
        mesh=mesh,
        in_specs=placed,
        out_specs=(
            P(None, "gx", "gy", None),
            P(None, "gx", "gy", None),
            P(None, None, None, ("gx", "gy")),
        ),
        check_vma=False,
    )
```

profile of v0, /device:TPU:1, one launch (start us, length us, event | category | flops | bytes accessed | tf_op | source)
XLA Modules:
  0.0 1662.4 jit_solution(8427986229018312662)
XLA Ops:
  25.7 29.2 %fusion.54 = (f32[8,1,16384]{2,1,0:T(1,128)S(1)}, f32[8,1,16384]{2,1,0:T(1,128)}, f32[8,1,16384]{2,1,0:T(1,128)}, f32[8,1,16384]{2,1,0:T(1,128)}, f32[8,1,16384]...) fusion(f32[8,8,16384]{2,1,0:T(8,128)} %get-tuple-element.77, ...), kind=kLoop, calls=%fused_computation.366 | loop fusion | bytes 16777216 | tf_op jit(solution)/shard_map/slice | solution.py:55
  92.8 17.5 %copy.189 = f32[3,16,16,256]{0,3,2,1:T(8,128)} copy(f32[3,16,16,256]{3,2,1,0:T(8,128)} %fusion.4) | data formatting | bytes 1572864 | tf_op jit(solution)/shard_map/add | solution.py:112
  110.4 38.5 %gather_fusion = f32[8192,3]{1,0:T(8,128)} fusion(f32[3,65536]{0,1:T(8,128)} %bitcast.608, s32[8192]{0:T(1024)S(1)} %broadcast_clamp_fusion), kind=kCustom, calls=%fused_computation | custom fusion | bytes 229376 | tf_op jit(solution)/shard_map/gather | solution.py:114
  253.2 61.6 %scatter_fusion.1 = f32[3,65536]{0,1:T(8,128)} fusion(f32[3,65536]{0,1:T(8,128)} %bitcast.609, s32[8192]{0:T(1024)S(1)} %bitcast.773, f32[8192,3]{1,0:T(8,128)} %copy.199), kind=kCustom, calls=%fused_computation.9 | custom fusion | flops 24576 | bytes 327680 | tf_op jit(solution)/shard_map/scatter-add | solution.py:136
  314.8 53.3 %slice_reduce_fusion.8 = (f32[65536]{0:T(1024)}, f32[65536]{0:T(1024)}, f32[65536]{0:T(1024)}) fusion(f32[3,65536]{0,1:T(8,128)} %scatter_fusion.1), kind=kLoop, calls=%fused_computation.24 | loop fusion | bytes 1572864 | tf_op jit(solution)/shard_map/slice | solution.py:38
  368.1 39.7 %slice_reduce_fusion.14 = (f32[61440]{0:T(1024)}, f32[61440]{0:T(1024)}) fusion(f32[3,65536]{0,1:T(8,128)} %scatter_fusion.1), kind=kLoop, calls=%fused_computation.30 | loop fusion | bytes 983040 | tf_op jit(solution)/shard_map/slice | solution.py:21
  407.8 17.5 %slice.1163 = f32[2,16,1,256]{0,3,2,1:T(8,128)} slice(f32[3,16,16,256]{0,3,2,1:T(8,128)} %bitcast.610), slice={[0:3:2], [0:16:1], [0:1:1], [0:256:1]} | slice | bytes 65536 | tf_op jit(solution)/shard_map/slice | solution.py:108
  441.8 18.3 %copy.202 = f32[3,65536]{1,0:T(4,128)} copy(f32[3,65536]{0,1:T(8,128)} %scatter_fusion.1) | data formatting | bytes 1572864 | tf_op jit(solution)/shard_map/scatter-add | solution.py:136
  501.0 16.4 copy.210
  517.4 38.4 %gather_fusion.2 = f32[8192,3]{1,0:T(8,128)} fusion(f32[3,65536]{0,1:T(8,128)} %copy.210, s32[8192]{0:T(1024)S(1)} %copy-done.120), kind=kCustom, calls=%fused_computation.2 | custom fusion | bytes 229376 | tf_op jit(solution)/shard_map/gather | solution.py:114
  609.5 24.1 %multiply_add_fusion.5 = (f32[1,8,8,16384]{3,2,1,0:T(8,128)}, f32[1,8,8,16384]{3,2,1,0:T(8,128)}, f32[1,8,8,16384]{3,2,1,0:T(8,128)}) fusion(f32[8,16384]{1,0:T(8,128)} %bitcast.679, f32[8,16384]{1,0:T(8,128)} %get-tuple-element.160, f32[8,16384]{1,0:T(8,128)} %bitcast.681, f32[8,16384]{1,0:T(8,128)} %get-tuple-element.161, f32[8,16384]{1,0:T(8,128)} %bitcast.683, ...), kind=kLoop, calls=%fused_computation.37 | loop fusion | flops 119537664 | bytes 46269696 | tf_op jit(solution)/shard_map/add | solution.py:69
  633.7 22.9 %multiply_add_fusion.10 = (f32[8,8,16384]{2,1,0:T(8,128)}, f32[8,8,16384]{2,1,0:T(8,128)S(1)}, f32[8,8,16384]{2,1,0:T(8,128)}) fusion(f32[8,8]{1,0:T(8,128)S(1)} %get-tuple-element.297, f32[8]{0:T(128)} %get-tuple-element.282, f32[8,16384]{1,0:T(8,128)} %bitcast.680, f32[8,16384]{1,0:T(8,128)} %get-tuple-element.160, f32[8]{0:T(128)} %get-tuple-element.37, ...), kind=kLoop, calls=%fused_computation.45 | loop fusion | flops 81788928 | bytes 42075392 | tf_op jit(solution)/shard_map/add | solution.py:69
  669.1 17.0 %fusion.52 = (f32[8,1,16384]{2,1,0:T(1,128)}, f32[8,1,16384]{2,1,0:T(1,128)}, f32[8,1,16384]{2,1,0:T(1,128)}, f32[8,1,16384]{2,1,0:T(1,128)}, f32[8,1,16384]{2,1...) fusion(f32[8,8,16384]{2,1,0:T(8,128)} %get-tuple-element.56), kind=kLoop, calls=%fused_computation.364 | loop fusion | bytes 8388608 | tf_op jit(solution)/shard_map/slice | solution.py:55
  707.8 61.6 %scatter_fusion.3 = f32[3,65536]{0,1:T(8,128)} fusion(f32[3,65536]{0,1:T(8,128)} %copy.210, s32[8192]{0:T(1024)} %bitcast.772, f32[8192,3]{1,0:T(8,128)} %copy.211), kind=kCustom, calls=%fused_computation.11 | custom fusion | flops 24576 | bytes 327680 | tf_op jit(solution)/shard_map/scatter-add | solution.py:136
  769.4 53.3 %slice_reduce_fusion.5 = (f32[65536]{0:T(1024)}, f32[65536]{0:T(1024)}, f32[65536]{0:T(1024)}) fusion(f32[3,65536]{0,1:T(8,128)} %scatter_fusion.3), kind=kLoop, calls=%fused_computation.21 | loop fusion | bytes 1572864 | tf_op jit(solution)/shard_map/slice | solution.py:38
  822.6 39.7 %slice_reduce_fusion.12 = (f32[61440]{0:T(1024)}, f32[61440]{0:T(1024)}) fusion(f32[3,65536]{0,1:T(8,128)} %scatter_fusion.3), kind=kLoop, calls=%fused_computation.28 | loop fusion | bytes 983040 | tf_op jit(solution)/shard_map/slice | solution.py:21
  862.4 17.5 %slice.1230 = f32[2,16,1,256]{0,3,2,1:T(8,128)} slice(f32[3,16,16,256]{0,3,2,1:T(8,128)} %bitcast.606), slice={[0:3:2], [0:16:1], [0:1:1], [0:256:1]} | slice | bytes 65536 | tf_op jit(solution)/shard_map/slice | solution.py:108
  897.0 18.3 %copy.214 = f32[3,65536]{1,0:T(4,128)} copy(f32[3,65536]{0,1:T(8,128)} %scatter_fusion.3) | data formatting | bytes 1572864 | tf_op jit(solution)/shard_map/scatter-add | solution.py:136
  956.5 16.4 copy.222
  972.9 41.1 %gather_fusion.4 = f32[8192,3]{1,0:T(8,128)} fusion(f32[3,65536]{0,1:T(8,128)} %copy.222, s32[8192]{0:T(1024)} %copy-done.119), kind=kCustom, calls=%fused_computation.4 | custom fusion | bytes 229376 | tf_op jit(solution)/shard_map/gather | solution.py:114
  1077.3 25.5 %multiply_add_fusion.9 = (f32[8,8,16384]{2,1,0:T(8,128)}, f32[8,8,16384]{2,1,0:T(8,128)}) fusion(f32[8,8,16384]{2,1,0:T(8,128)} %get-tuple-element.56, f32[8,16384]{1,0:T(8,128)} %bitcast.647, f32[8,16384]{1,0:T(8,128)} %get-tuple-element.144, f32[8,16384]{1,0:T(8,128)} %bitcast.649, f32[8,16384]{1,0:T(8,128)} %get-tuple-element.145, ...), kind=kLoop, calls=%fused_computation.42 | loop fusion | flops 119537664 | bytes 50529280 | tf_op jit(solution)/shard_map/add | solution.py:69
  1102.8 16.8 %fusion.50 = (f32[8,1,16384]{2,1,0:T(1,128)S(1)}, f32[8,1,16384]{2,1,0:T(1,128)S(1)}, f32[8,1,16384]{2,1,0:T(1,128)S(1)}, f32[8,1,16384]{2,1,0:T(1,128)S(1)}, f3...) fusion(f32[8,8,16384]{2,1,0:T(8,128)} %get-tuple-element.53), kind=kLoop, calls=%fused_computation.362 | loop fusion | bytes 8388608 | tf_op jit(solution)/shard_map/slice | solution.py:55
  1144.8 17.5 %fusion.49 = (f32[8,1,16384]{2,1,0:T(1,128)}, f32[8,1,16384]{2,1,0:T(1,128)}, f32[8,1,16384]{2,1,0:T(1,128)}, f32[8,1,16384]{2,1,0:T(1,128)}, f32[8,1,16384]{2,1...) fusion(f32[8,8,16384]{2,1,0:T(8,128)} %get-tuple-element.52), kind=kLoop, calls=%fused_computation.361 | loop fusion | bytes 8388608 | tf_op jit(solution)/shard_map/slice | solution.py:55
  1166.5 61.4 %scatter_fusion.5 = f32[3,65536]{0,1:T(8,128)} fusion(f32[3,65536]{0,1:T(8,128)} %copy.222, s32[8192]{0:T(1024)S(1)} %bitcast.774, f32[8192,3]{1,0:T(8,128)} %copy.223), kind=kCustom, calls=%fused_computation.13 | custom fusion | flops 24576 | bytes 327680 | tf_op jit(solution)/shard_map/scatter-add | solution.py:136
  1228.0 53.3 %slice_reduce_fusion.2 = (f32[65536]{0:T(1024)}, f32[65536]{0:T(1024)S(1)}, f32[65536]{0:T(1024)S(1)}) fusion(f32[3,65536]{0,1:T(8,128)} %scatter_fusion.5), kind=kLoop, calls=%fused_computation.18 | loop fusion | bytes 1572864 | tf_op jit(solution)/shard_map/slice | solution.py:38
  1281.3 39.7 %slice_reduce_fusion.10 = (f32[61440]{0:T(1024)}, f32[61440]{0:T(1024)}) fusion(f32[3,65536]{0,1:T(8,128)} %scatter_fusion.5), kind=kLoop, calls=%fused_computation.26 | loop fusion | bytes 983040 | tf_op jit(solution)/shard_map/slice | solution.py:21
  1345.0 18.3 %copy.226 = f32[3,65536]{1,0:T(4,128)} copy(f32[3,65536]{0,1:T(8,128)} %scatter_fusion.5) | data formatting | bytes 1572864 | tf_op jit(solution)/shard_map/scatter-add | solution.py:136
  1397.0 16.1 copy.234
  1413.1 38.4 %gather_fusion.6 = f32[8192,3]{1,0:T(8,128)} fusion(f32[3,65536]{0,1:T(8,128)} %copy.234, s32[8192]{0:T(1024)S(1)} %copy-done.121), kind=kCustom, calls=%fused_computation.6 | custom fusion | bytes 229376 | tf_op jit(solution)/shard_map/gather | solution.py:114
  1528.2 33.7 %multiply_add_fusion.1 = (f32[1,8,8,16384]{3,2,1,0:T(8,128)S(1)}, f32[1,8,8,16384]{3,2,1,0:T(8,128)S(1)}, f32[1,8,8,16384]{3,2,1,0:T(8,128)S(1)}) fusion(f32[8,16384]{1,0:T(8,128)} %bitcast.728, f32[8,16384]{1,0:T(8,128)} %copy-done.33, f32[8,16384]{1,0:T(8,128)} %bitcast.730, f32[8,16384]{1,0:T(8,128)} %copy-done.34, f32[8,16384]{1,0:T(8,128)} %bitcast.732, ...), kind=kLoop, calls=%fused_computation.33 | loop fusion | flops 159383552 | bytes 58918144 | tf_op jit(solution)/shard_map/add | solution.py:69
  1580.5 61.4 %scatter_fusion.7 = f32[3,65536]{0,1:T(8,128)} fusion(f32[3,65536]{0,1:T(8,128)} %copy.234, s32[8192]{0:T(1024)S(1)} %bitcast.775, f32[8192,3]{1,0:T(8,128)} %copy.235), kind=kCustom, calls=%fused_computation.15 | custom fusion | flops 24576 | bytes 327680 | tf_op jit(solution)/shard_map/scatter-add | solution.py:136
  1642.0 20.2 %copy.236 = f32[3,16,16,256]{3,2,1,0:T(8,128)} copy(f32[3,16,16,256]{0,3,2,1:T(8,128)} %bitcast.614) | data formatting | bytes 1572864
  (669 shorter events, 614.3 us)
Async XLA Ops:
  2.2 75.7 %collective-permute-start = (f32[2,16,1,256]{3,2,1,0:T(1,128)}, f32[2,16,1,256]{3,2,1,0:T(1,128)}, u32[]{:S(2)}, u32[]{:S(2)}) collective-permute-start(f32[2,16,1,256]{3,2,1,0:T(1,128)} %slice.1091), channel_id=1, source_target_pairs={{1,0},{2,1},{3,2},{4,3},{5,4},{6,5},{7,6},{9,8},{10,9},{11,10},{12... | collective-permute-start | bytes 98312 | tf_op jit(solution)/shard_map/ppermute | solution.py:15
  4.9 73.7 %collective-permute-start.1 = (f32[2,1,16,256]{3,2,1,0:T(8,128)}, f32[2,1,16,256]{3,2,1,0:T(8,128)}, u32[]{:S(2)}, u32[]{:S(2)}) collective-permute-start(f32[2,1,16,256]{3,2,1,0:T(8,128)} %slice.1099), channel_id=1, source_target_pairs={{8,0},{16,8},{24,16},{32,24},{40,32},{48,40},{56,48},{64,56},{72,6... | collective-permute-start | bytes 98312 | tf_op jit(solution)/shard_map/ppermute | solution.py:15
  22.4 88.0 %copy-start.119 = (s32[8192]{0:T(1024)}, s32[8192]{0:T(1024)S(1)}, u32[]{:S(2)}) copy-start(s32[8192]{0:T(1024)S(1)} %broadcast_clamp_fusion) | copy-start | bytes 98308
  23.8 174.6 %copy-start.106 = (f32[1,16384]{1,0:T(1,128)}, f32[1,16384]{1,0:T(1,128)S(1)}, u32[]{:S(2)}) copy-start(f32[1,16384]{1,0:T(1,128)S(1)} %get-tuple-element.244) | copy-start | bytes 196612
  80.7 10.1 collective-permute-start.2
  87.0 4.4 collective-permute-start.3
  110.4 43.0 %copy-start.158 = (s32[128]{0:T(128)S(1)}, s32[128]{0:T(128)}, u32[]{:S(2)}) copy-start(s32[128]{0:T(128)} %copy-done.157) | copy-start | bytes 1540
  172.7 24.4 %all-to-all-start = ((f32[3,128,128]{2,0,1:T(4,128)}), f32[3,128,128]{2,0,1:T(4,128)}, u32[]{:S(2)}, u32[]{:S(2)}) async-start(f32[3,128,128]{2,0,1:T(4,128)} %copy.194), calls=%async_computation | async-start | bytes 524288 | tf_op jit(solution)/shard_map/all_to_all | solution.py:120
  214.4 23.8 %all-to-all-start.1 = ((f32[3,128,128]{2,0,1:T(4,128)}), f32[3,128,128]{2,0,1:T(4,128)}, u32[]{:S(2)}, u32[]{:S(2)}) async-start(f32[3,128,128]{2,0,1:T(4,128)} %multiply_bitcast_fusion.3), calls=%async_computation.1 | async-start | bytes 524288 | tf_op jit(solution)/shard_map/all_to_all | solution.py:126
  427.5 47.3 %collective-permute-start.4 = (f32[2,16,1,256]{3,2,1,0:T(1,128)S(1)}, f32[2,16,1,256]{3,2,1,0:T(1,128)}, u32[]{:S(2)}, u32[]{:S(2)}) collective-permute-start(f32[2,16,1,256]{3,2,1,0:T(1,128)S(1)} %copy.301), channel_id=1, source_target_pairs={{1,0},{2,1},{3,2},{4,3},{5,4},{6,5},{7,6},{9,8},{10,9},{11,10},{12... | collective-permute-start | bytes 98312 | tf_op jit(solution)/shard_map/ppermute | solution.py:15
  462.9 12.6 collective-permute-start.5
  480.9 8.9 collective-permute-start.6
  487.0 3.8 collective-permute-start.7
  517.4 42.9 %copy-start.159 = (s32[128]{0:T(128)S(1)}, s32[128]{0:T(128)}, u32[]{:S(2)}) copy-start(s32[128]{0:T(128)} %copy-done.157) | copy-start | bytes 1540
  579.6 27.5 %all-to-all-start.2 = ((f32[3,128,128]{2,0,1:T(4,128)}), f32[3,128,128]{2,0,1:T(4,128)}, u32[]{:S(2)}, u32[]{:S(2)}) async-start(f32[3,128,128]{2,0,1:T(4,128)} %copy.206), calls=%async_computation.2 | async-start | bytes 524288 | tf_op jit(solution)/shard_map/all_to_all | solution.py:120
  658.3 34.5 %all-to-all-start.3 = ((f32[3,128,128]{2,0,1:T(4,128)}), f32[3,128,128]{2,0,1:T(4,128)}, u32[]{:S(2)}, u32[]{:S(2)}) async-start(f32[3,128,128]{2,0,1:T(4,128)} %multiply_bitcast_fusion.2), calls=%async_computation.3 | async-start | bytes 524288 | tf_op jit(solution)/shard_map/all_to_all | solution.py:126
  882.7 47.2 %collective-permute-start.8 = (f32[2,16,1,256]{3,2,1,0:T(1,128)}, f32[2,16,1,256]{3,2,1,0:T(1,128)}, u32[]{:S(2)}, u32[]{:S(2)}) collective-permute-start(f32[2,16,1,256]{3,2,1,0:T(1,128)} %copy.303), channel_id=1, source_target_pairs={{1,0},{2,1},{3,2},{4,3},{5,4},{6,5},{7,6},{9,8},{10,9},{11,10},{12... | collective-permute-start | bytes 98312 | tf_op jit(solution)/shard_map/ppermute | solution.py:15
  918.1 12.7 collective-permute-start.9
  936.5 8.9 collective-permute-start.10
  942.3 4.0 collective-permute-start.11
  1037.9 36.5 %all-to-all-start.4 = ((f32[3,128,128]{2,0,1:T(4,128)}), f32[3,128,128]{2,0,1:T(4,128)}, u32[]{:S(2)}, u32[]{:S(2)}) async-start(f32[3,128,128]{2,0,1:T(4,128)} %copy.218), calls=%async_computation.4 | async-start | bytes 524288 | tf_op jit(solution)/shard_map/all_to_all | solution.py:120
  1135.1 27.2 %all-to-all-start.5 = ((f32[3,128,128]{2,0,1:T(4,128)}), f32[3,128,128]{2,0,1:T(4,128)S(1)}, u32[]{:S(2)}, u32[]{:S(2)}) async-start(f32[3,128,128]{2,0,1:T(4,128)} %multiply_bitcast_fusion.1), calls=%async_computation.5 | async-start | bytes 524288 | tf_op jit(solution)/shard_map/all_to_all | solution.py:126
  1336.8 38.9 %collective-permute-start.12 = (f32[2,16,1,256]{3,2,1,0:T(1,128)S(1)}, f32[2,16,1,256]{3,2,1,0:T(1,128)}, u32[]{:S(2)}, u32[]{:S(2)}) collective-permute-start(f32[2,16,1,256]{3,2,1,0:T(1,128)S(1)} %copy.305), channel_id=1, source_target_pairs={{1,0},{2,1},{3,2},{4,3},{5,4},{6,5},{7,6},{9,8},{10,9},{11,10},{12... | collective-permute-start | bytes 98312 | tf_op jit(solution)/shard_map/ppermute | solution.py:15
  1366.2 10.2 collective-permute-start.13
  1381.6 8.9 collective-permute-start.14
  1387.6 3.9 collective-permute-start.15
  1413.1 41.5 %copy-start.160 = (s32[128]{0:T(128)S(1)}, s32[128]{0:T(128)}, u32[]{:S(2)}) copy-start(s32[128]{0:T(128)} %copy-done.157) | copy-start | bytes 1540
  1459.9 27.1 %all-to-all-start.6 = ((f32[3,128,128]{2,0,1:T(4,128)}), f32[3,128,128]{2,0,1:T(4,128)}, u32[]{:S(2)}, u32[]{:S(2)}) async-start(f32[3,128,128]{2,0,1:T(4,128)} %copy.230), calls=%async_computation.6 | async-start | bytes 524288 | tf_op jit(solution)/shard_map/all_to_all | solution.py:120
  1517.9 58.5 %all-to-all-start.7 = ((f32[3,128,128]{2,0,1:T(4,128)}), f32[3,128,128]{2,0,1:T(4,128)S(1)}, u32[]{:S(2)}, u32[]{:S(2)}) async-start(f32[3,128,128]{2,0,1:T(4,128)} %multiply_bitcast_fusion), calls=%async_computation.7 | async-start | bytes 524288 | tf_op jit(solution)/shard_map/all_to_all | solution.py:126
  1528.0 34.0 %copy-start.60 = (f32[8,16384]{1,0:T(8,128)S(1)}, f32[8,16384]{1,0:T(8,128)}, u32[]{:S(2)}) copy-start(f32[8,16384]{1,0:T(8,128)} %get-tuple-element.79) | copy-start | bytes 1572868
  1528.1 34.0 %copy-start.61 = (f32[8,16384]{1,0:T(8,128)S(1)}, f32[8,16384]{1,0:T(8,128)}, u32[]{:S(2)}) copy-start(f32[8,16384]{1,0:T(8,128)} %get-tuple-element.80) | copy-start | bytes 1572868
  1528.1 34.0 %copy-start.62 = (f32[8,16384]{1,0:T(8,128)S(1)}, f32[8,16384]{1,0:T(8,128)}, u32[]{:S(2)}) copy-start(f32[8,16384]{1,0:T(8,128)} %get-tuple-element.81) | copy-start | bytes 1572868
  (157 other events, 1875.2 us)
where the time goes:
time: 1680 us; the launch traced here: 1660 us
  local copies, waits for them, and re-layouts  1040 us (62%)
  other arithmetic  454 us (27%)
  starting transfers between devices  148 us (9%)
    scatter-add x4, other arithmetic, body(): flattened = flattened.at[:, positions].add(-back_terms)  246 us
    slice x3, local copies, waits for them, and re-layouts, curl_ahead(): fields[2]  160 us
    gather x4, local copies, waits for them, and re-layouts, body(): samples = flattened[:, positions].reshape(3, tile_count, per_tile)  156 us
    slice x19, local copies, waits for them, and re-layouts, forward(): lax.slice_in_dim(values_in, 1, length, axis=along)  138 us
    unnamed x406, local copies, waits for them, and re-layouts  114 us
    slice x7, local copies, waits for them, and re-layouts, commutator(): matrix[:, inner][:, None, :] * symmetric[inner][None, :, None]  93.7 us
    add x3, other arithmetic, advance_driven(): real_part + time_step * change_real  80.8 us
    add x4, local copies, waits for them, and re-layouts, body(): field_e + courant * curl_behind(field_h, behind_planes, behind_rows)  66.3 us
  transfers between devices with their start and end apart: 24, of which 5 were waited for; matrix products, arithmetic and copies ran while one was open for 21% of the time, Pallas kernels for 0%

commit v1 on v0

--- a/solution.py
+++ b/solution.py
@@ -123,12 +123,18 @@
         density, feed_terms = advance(
             density, dipole, incoming.reshape(3, -1), levels, symmetric, damping
         )
-        returned = lax.all_to_all(
-            feed_terms.reshape(3, devices, -1),
-            ("gx", "gy"),
-            split_axis=1,
-            concat_axis=1,
-            tiled=True,
+        returned = jnp.concatenate(
+            lax.all_to_all(
+                jnp.stack(
+                    jnp.split(
+                        feed_terms.reshape(3, devices, -1), lax.axis_size(("gx", "gy")), axis=1
+                    )
+                ),
+                ("gx", "gy"),
+                0,
+                0,
+            ),
+            axis=1,
         )
         back_terms = returned.reshape(3, devices * capacity, per_tile)[:, slot_rows, :].reshape(
             3, -1

time: 1680 us -> 1970 us (1.17)
  local copies, waits for them, and re-layouts: 1040 us -> 1330 us
    unnamed x406 -> x918, local copies, waits for them, and re-layouts: 114 us -> 402 us
  transfers between devices with their start and end apart: 24 -> 24, of which waited for: 5 -> 5; matrix products, arithmetic and copies ran while one was open for 21% -> 18% of each run, Pallas kernels for 0% -> 0%
where the time goes in v1:
time: 1970 us; the launch traced here: 1950 us
  local copies, waits for them, and re-layouts  1330 us (68%)
  other arithmetic  452 us (23%)
  starting transfers between devices  147 us (7%)
    unnamed x918, local copies, waits for them, and re-layouts  402 us
    scatter-add x4, other arithmetic, body(): flattened = flattened.at[:, positions].add(-back_terms)  247 us
    slice x3, local copies, waits for them, and re-layouts, curl_ahead(): fields[2]  160 us
    gather x4, local copies, waits for them, and re-layouts, body(): samples = flattened[:, positions].reshape(3, tile_count, per_tile)  156 us
    slice x19, local copies, waits for them, and re-layouts, forward(): lax.slice_in_dim(values_in, 1, length, axis=along)  138 us
    slice x7, local copies, waits for them, and re-layouts, commutator(): matrix[:, inner][:, None, :] * symmetric[inner][None, :, None]  93.9 us
    add x3, other arithmetic, advance_driven(): real_part + time_step * change_real  80.8 us
    add x4, local copies, waits for them, and re-layouts, body(): field_e + courant * curl_behind(field_h, behind_planes, behind_rows)  66.3 us
  transfers between devices with their start and end apart: 24, of which 5 were waited for; matrix products, arithmetic and copies ran while one was open for 18% of the time, Pallas kernels for 0%

profile of v1, /device:TPU:1, one launch (start us, length us, event | category | flops | bytes accessed | tf_op | source)
XLA Modules:
  0.0 1950.3 jit_solution(13220759029409034266)
XLA Ops:
  25.7 29.2 %fusion.54 = (f32[8,1,16384]{2,1,0:T(1,128)S(1)}, f32[8,1,16384]{2,1,0:T(1,128)}, f32[8,1,16384]{2,1,0:T(1,128)}, f32[8,1,16384]{2,1,0:T(1,128)}, f32[8,1,16384]...) fusion(f32[8,8,16384]{2,1,0:T(8,128)} %get-tuple-element.80, ...), kind=kLoop, calls=%fused_computation.1394 | loop fusion | bytes 16777216 | tf_op jit(solution)/shard_map/slice | solution.py:55
  92.9 17.5 copy.1250
  110.4 38.5 %gather_fusion = f32[8192,3]{1,0:T(8,128)} fusion(f32[3,65536]{0,1:T(8,128)} %bitcast.2688, s32[8192]{0:T(1024)S(1)} %broadcast_clamp_fusion), kind=kCustom, calls=%fused_computation | custom fusion | bytes 229376 | tf_op jit(solution)/shard_map/gather | solution.py:114
  324.9 61.8 %scatter_fusion.1 = f32[3,65536]{0,1:T(8,128)} fusion(f32[3,65536]{0,1:T(8,128)} %bitcast.2689, s32[8192]{0:T(1024)S(1)} %bitcast.2853, f32[8192,3]{1,0:T(8,128)} %copy.1260), kind=kCustom, calls=%fused_computation.9 | custom fusion | flops 24576 | bytes 327680 | tf_op jit(solution)/shard_map/scatter-add | solution.py:142
  386.7 53.3 %slice_reduce_fusion.8 = (f32[65536]{0:T(1024)}, f32[65536]{0:T(1024)}, f32[65536]{0:T(1024)}) fusion(f32[3,65536]{0,1:T(8,128)} %scatter_fusion.1), kind=kLoop, calls=%fused_computation.24 | loop fusion | bytes 1572864 | tf_op jit(solution)/shard_map/slice | solution.py:38
  440.0 39.7 %slice_reduce_fusion.14 = (f32[61440]{0:T(1024)}, f32[61440]{0:T(1024)}) fusion(f32[3,65536]{0,1:T(8,128)} %scatter_fusion.1), kind=kLoop, calls=%fused_computation.30 | loop fusion | bytes 983040 | tf_op jit(solution)/shard_map/slice | solution.py:21
  479.7 17.5 slice.1163
  513.8 18.3 copy.1263
  572.9 16.4 copy.1271
  589.3 38.4 %gather_fusion.2 = f32[8192,3]{1,0:T(8,128)} fusion(f32[3,65536]{0,1:T(8,128)} %copy.1271, s32[8192]{0:T(1024)S(1)} %copy-done.120), kind=kCustom, calls=%fused_computation.2 | custom fusion | bytes 229376 | tf_op jit(solution)/shard_map/gather | solution.py:114
  681.4 24.1 %multiply_add_fusion.5 = (f32[1,8,8,16384]{3,2,1,0:T(8,128)}, f32[1,8,8,16384]{3,2,1,0:T(8,128)}, f32[1,8,8,16384]{3,2,1,0:T(8,128)}) fusion(f32[8,16384]{1,0:T(8,128)} %bitcast.2759, f32[8,16384]{1,0:T(8,128)} %get-tuple-element.163, f32[8,16384]{1,0:T(8,128)} %bitcast.2761, f32[8,16384]{1,0:T(8,128)} %get-tuple-element.164, f32[8,16384]{1,0:T(8,128)} %bitcast.2763, ...), kind=kLoop, calls=%fused_computation.37 | loop fusion | flops 119537664 | bytes 46269696 | tf_op jit(solution)/shard_map/add | solution.py:69
  705.5 22.9 %multiply_add_fusion.10 = (f32[8,8,16384]{2,1,0:T(8,128)}, f32[8,8,16384]{2,1,0:T(8,128)S(1)}, f32[8,8,16384]{2,1,0:T(8,128)}) fusion(f32[8,8]{1,0:T(8,128)S(1)} %get-tuple-element.300, f32[8]{0:T(128)} %get-tuple-element.285, f32[8,16384]{1,0:T(8,128)} %bitcast.2760, f32[8,16384]{1,0:T(8,128)} %get-tuple-element.163, f32[8]{0:T(128)} %get-tuple-element.40, ...), kind=kLoop, calls=%fused_computation.45 | loop fusion | flops 81788928 | bytes 42075392 | tf_op jit(solution)/shard_map/add | solution.py:69
  812.5 16.9 fusion.52
  851.1 61.8 %scatter_fusion.3 = f32[3,65536]{0,1:T(8,128)} fusion(f32[3,65536]{0,1:T(8,128)} %copy.1271, s32[8192]{0:T(1024)} %bitcast.2852, f32[8192,3]{1,0:T(8,128)} %copy.1272), kind=kCustom, calls=%fused_computation.11 | custom fusion | flops 24576 | bytes 327680 | tf_op jit(solution)/shard_map/scatter-add | solution.py:142
  912.9 53.3 %slice_reduce_fusion.5 = (f32[65536]{0:T(1024)}, f32[65536]{0:T(1024)}, f32[65536]{0:T(1024)}) fusion(f32[3,65536]{0,1:T(8,128)} %scatter_fusion.3), kind=kLoop, calls=%fused_computation.21 | loop fusion | bytes 1572864 | tf_op jit(solution)/shard_map/slice | solution.py:38
  966.2 39.7 %slice_reduce_fusion.12 = (f32[61440]{0:T(1024)}, f32[61440]{0:T(1024)}) fusion(f32[3,65536]{0,1:T(8,128)} %scatter_fusion.3), kind=kLoop, calls=%fused_computation.28 | loop fusion | bytes 983040 | tf_op jit(solution)/shard_map/slice | solution.py:21
  1006.0 17.5 slice.1230
  1040.7 18.3 copy.1275
  1100.0 16.4 copy.1283
  1116.4 41.1 %gather_fusion.4 = f32[8192,3]{1,0:T(8,128)} fusion(f32[3,65536]{0,1:T(8,128)} %copy.1283, s32[8192]{0:T(1024)} %copy-done.119), kind=kCustom, calls=%fused_computation.4 | custom fusion | bytes 229376 | tf_op jit(solution)/shard_map/gather | solution.py:114
  1220.8 25.5 %multiply_add_fusion.9 = (f32[8,8,16384]{2,1,0:T(8,128)}, f32[8,8,16384]{2,1,0:T(8,128)}) fusion(f32[8,8,16384]{2,1,0:T(8,128)} %get-tuple-element.59, f32[8,16384]{1,0:T(8,128)} %bitcast.2727, f32[8,16384]{1,0:T(8,128)} %get-tuple-element.147, f32[8,16384]{1,0:T(8,128)} %bitcast.2729, f32[8,16384]{1,0:T(8,128)} %get-tuple-element.148, ...), kind=kLoop, calls=%fused_computation.42 | loop fusion | flops 119537664 | bytes 50529280 | tf_op jit(solution)/shard_map/add | solution.py:69
  1246.2 17.1 fusion.50
  1360.2 17.5 fusion.49
  1381.9 61.4 %scatter_fusion.5 = f32[3,65536]{0,1:T(8,128)} fusion(f32[3,65536]{0,1:T(8,128)} %copy.1283, s32[8192]{0:T(1024)S(1)} %bitcast.2854, f32[8192,3]{1,0:T(8,128)} %copy.1284), kind=kCustom, calls=%fused_computation.13 | custom fusion | flops 24576 | bytes 327680 | tf_op jit(solution)/shard_map/scatter-add | solution.py:142
  1443.4 53.3 %slice_reduce_fusion.2 = (f32[65536]{0:T(1024)}, f32[65536]{0:T(1024)S(1)}, f32[65536]{0:T(1024)S(1)}) fusion(f32[3,65536]{0,1:T(8,128)} %scatter_fusion.5), kind=kLoop, calls=%fused_computation.18 | loop fusion | bytes 1572864 | tf_op jit(solution)/shard_map/slice | solution.py:38
  1496.6 39.7 %slice_reduce_fusion.10 = (f32[61440]{0:T(1024)}, f32[61440]{0:T(1024)}) fusion(f32[3,65536]{0,1:T(8,128)} %scatter_fusion.5), kind=kLoop, calls=%fused_computation.26 | loop fusion | bytes 983040 | tf_op jit(solution)/shard_map/slice | solution.py:21
  1560.3 18.3 copy.1287
  1611.9 16.1 copy.1295
  1628.0 38.4 %gather_fusion.6 = f32[8192,3]{1,0:T(8,128)} fusion(f32[3,65536]{0,1:T(8,128)} %copy.1295, s32[8192]{0:T(1024)S(1)} %copy-done.121), kind=kCustom, calls=%fused_computation.6 | custom fusion | bytes 229376 | tf_op jit(solution)/shard_map/gather | solution.py:114
  1816.2 33.7 %multiply_add_fusion.1 = (f32[1,8,8,16384]{3,2,1,0:T(8,128)S(1)}, f32[1,8,8,16384]{3,2,1,0:T(8,128)S(1)}, f32[1,8,8,16384]{3,2,1,0:T(8,128)S(1)}) fusion(f32[8,16384]{1,0:T(8,128)} %bitcast.2808, f32[8,16384]{1,0:T(8,128)} %copy-done.33, f32[8,16384]{1,0:T(8,128)} %bitcast.2810, f32[8,16384]{1,0:T(8,128)} %copy-done.34, f32[8,16384]{1,0:T(8,128)} %bitcast.2812, ...), kind=kLoop, calls=%fused_computation.33 | loop fusion | flops 159383552 | bytes 58918144 | tf_op jit(solution)/shard_map/add | solution.py:69
  1868.4 61.4 %scatter_fusion.7 = f32[3,65536]{0,1:T(8,128)} fusion(f32[3,65536]{0,1:T(8,128)} %copy.1295, s32[8192]{0:T(1024)S(1)} %bitcast.2855, f32[8192,3]{1,0:T(8,128)} %copy.1296), kind=kCustom, calls=%fused_computation.15 | custom fusion | flops 24576 | bytes 327680 | tf_op jit(solution)/shard_map/scatter-add | solution.py:142
  1929.9 20.2 %copy.1297 = f32[3,16,16,256]{3,2,1,0:T(8,128)} copy(f32[3,16,16,256]{0,3,2,1:T(8,128)} %bitcast.2694) | data formatting | bytes 1572864
  (1185 shorter events, 901.2 us)
Async XLA Ops:
  2.2 75.7 %collective-permute-start = (f32[2,16,1,256]{3,2,1,0:T(1,128)}, f32[2,16,1,256]{3,2,1,0:T(1,128)}, u32[]{:S(2)}, u32[]{:S(2)}) collective-permute-start(f32[2,16,1,256]{3,2,1,0:T(1,128)} %slice.1091), channel_id=1, source_target_pairs={{1,0},{2,1},{3,2},{4,3},{5,4},{6,5},{7,6},{9,8},{10,9},{11,10},{12... | collective-permute-start | bytes 98312 | tf_op jit(solution)/shard_map/ppermute | solution.py:15
  4.9 73.8 %collective-permute-start.1 = (f32[2,1,16,256]{3,2,1,0:T(8,128)}, f32[2,1,16,256]{3,2,1,0:T(8,128)}, u32[]{:S(2)}, u32[]{:S(2)}) collective-permute-start(f32[2,1,16,256]{3,2,1,0:T(8,128)} %slice.1099), channel_id=1, source_target_pairs={{8,0},{16,8},{24,16},{32,24},{40,32},{48,40},{56,48},{64,56},{72,6... | collective-permute-start | bytes 98312 | tf_op jit(solution)/shard_map/ppermute | solution.py:15
  23.9 174.5 %copy-start.106 = (f32[1,16384]{1,0:T(1,128)}, f32[1,16384]{1,0:T(1,128)S(1)}, u32[]{:S(2)}) copy-start(f32[1,16384]{1,0:T(1,128)S(1)} %get-tuple-element.247) | copy-start | bytes 196612
  80.8 9.8 collective-permute-start.2
  87.1 4.4 collective-permute-start.3
  172.7 24.2 %all-to-all-start = ((f32[3,128,128]{2,0,1:T(4,128)}), f32[3,128,128]{2,0,1:T(4,128)}, u32[]{:S(2)}, u32[]{:S(2)}) async-start(f32[3,128,128]{2,0,1:T(4,128)} %copy.1255), calls=%async_computation | async-start | bytes 524288 | tf_op jit(solution)/shard_map/all_to_all | solution.py:120
  286.0 23.9 %all-to-all-start.1 = ((f32[128,3,1,128]{3,2,1,0:T(1,128)}), f32[128,3,1,128]{3,2,1,0:T(1,128)}, u32[]{:S(2)}, u32[]{:S(2)}) async-start(f32[128,3,1,128]{3,2,1,0:T(1,128)} %constant_dynamic-update-slice_fusion), calls=%async_computation.1 | async-start | bytes 393216 | tf_op jit(solution)/shard_map/all_to_all | solution.py:127
  499.4 47.2 %collective-permute-start.4 = (f32[2,16,1,256]{3,2,1,0:T(1,128)S(1)}, f32[2,16,1,256]{3,2,1,0:T(1,128)}, u32[]{:S(2)}, u32[]{:S(2)}) collective-permute-start(f32[2,16,1,256]{3,2,1,0:T(1,128)S(1)} %copy.1362), channel_id=1, source_target_pairs={{1,0},{2,1},{3,2},{4,3},{5,4},{6,5},{7,6},{9,8},{10,9},{11,10},{12... | collective-permute-start | bytes 98312 | tf_op jit(solution)/shard_map/ppermute | solution.py:15
  534.9 12.6 collective-permute-start.5
  552.9 8.9 collective-permute-start.6
  558.9 3.9 collective-permute-start.7
  651.5 27.4 %all-to-all-start.2 = ((f32[3,128,128]{2,0,1:T(4,128)}), f32[3,128,128]{2,0,1:T(4,128)}, u32[]{:S(2)}, u32[]{:S(2)}) async-start(f32[3,128,128]{2,0,1:T(4,128)} %copy.1267), calls=%async_computation.2 | async-start | bytes 524288 | tf_op jit(solution)/shard_map/all_to_all | solution.py:120
  801.9 34.2 %all-to-all-start.3 = ((f32[128,3,1,128]{3,2,1,0:T(1,128)}), f32[128,3,1,128]{3,2,1,0:T(1,128)}, u32[]{:S(2)}, u32[]{:S(2)}) async-start(f32[128,3,1,128]{3,2,1,0:T(1,128)} %constant_dynamic-update-slice_fusion.128), calls=%async_computation.3 | async-start | bytes 393216 | tf_op jit(solution)/shard_map/all_to_all | solution.py:127
  1026.3 47.1 %collective-permute-start.8 = (f32[2,16,1,256]{3,2,1,0:T(1,128)}, f32[2,16,1,256]{3,2,1,0:T(1,128)}, u32[]{:S(2)}, u32[]{:S(2)}) collective-permute-start(f32[2,16,1,256]{3,2,1,0:T(1,128)} %copy.1364), channel_id=1, source_target_pairs={{1,0},{2,1},{3,2},{4,3},{5,4},{6,5},{7,6},{9,8},{10,9},{11,10},{12... | collective-permute-start | bytes 98312 | tf_op jit(solution)/shard_map/ppermute | solution.py:15
  1061.8 12.5 collective-permute-start.9
  1080.0 8.9 collective-permute-start.10
  1085.8 4.0 collective-permute-start.11
  1181.4 36.4 %all-to-all-start.4 = ((f32[3,128,128]{2,0,1:T(4,128)}), f32[3,128,128]{2,0,1:T(4,128)}, u32[]{:S(2)}, u32[]{:S(2)}) async-start(f32[3,128,128]{2,0,1:T(4,128)} %copy.1279), calls=%async_computation.4 | async-start | bytes 524288 | tf_op jit(solution)/shard_map/all_to_all | solution.py:120
  1350.4 27.2 %all-to-all-start.5 = ((f32[128,3,1,128]{3,2,1,0:T(1,128)}), f32[128,3,1,128]{3,2,1,0:T(1,128)S(1)}, u32[]{:S(2)}, u32[]{:S(2)}) async-start(f32[128,3,1,128]{3,2,1,0:T(1,128)} %constant_dynamic-update-slice_fusion.256), calls=%async_computation.5 | async-start | bytes 393216 | tf_op jit(solution)/shard_map/all_to_all | solution.py:127
  1552.1 38.4 %collective-permute-start.12 = (f32[2,16,1,256]{3,2,1,0:T(1,128)S(1)}, f32[2,16,1,256]{3,2,1,0:T(1,128)}, u32[]{:S(2)}, u32[]{:S(2)}) collective-permute-start(f32[2,16,1,256]{3,2,1,0:T(1,128)S(1)} %copy.1366), channel_id=1, source_target_pairs={{1,0},{2,1},{3,2},{4,3},{5,4},{6,5},{7,6},{9,8},{10,9},{11,10},{12... | collective-permute-start | bytes 98312 | tf_op jit(solution)/shard_map/ppermute | solution.py:15
  1581.6 9.7 collective-permute-start.13
  1596.6 8.9 collective-permute-start.14
  1602.5 3.9 collective-permute-start.15
  1674.8 27.3 %all-to-all-start.6 = ((f32[3,128,128]{2,0,1:T(4,128)}), f32[3,128,128]{2,0,1:T(4,128)}, u32[]{:S(2)}, u32[]{:S(2)}) async-start(f32[3,128,128]{2,0,1:T(4,128)} %copy.1291), calls=%async_computation.6 | async-start | bytes 524288 | tf_op jit(solution)/shard_map/all_to_all | solution.py:120
  1725.5 90.4 %copy-start.19 = (f32[8,16384]{1,0:T(8,128)S(1)}, f32[8,16384]{1,0:T(8,128)}, u32[]{:S(2)}) copy-start(f32[8,16384]{1,0:T(8,128)} %get-tuple-element.131) | copy-start | bytes 1572868
  1725.5 90.4 %copy-start.20 = (f32[8,16384]{1,0:T(8,128)S(1)}, f32[8,16384]{1,0:T(8,128)}, u32[]{:S(2)}) copy-start(f32[8,16384]{1,0:T(8,128)} %get-tuple-element.132) | copy-start | bytes 1572868
  1725.5 90.4 %copy-start.21 = (f32[8,16384]{1,0:T(8,128)S(1)}, f32[8,16384]{1,0:T(8,128)}, u32[]{:S(2)}) copy-start(f32[8,16384]{1,0:T(8,128)} %get-tuple-element.133) | copy-start | bytes 1572868
  1725.6 90.4 %copy-start.22 = (f32[8,16384]{1,0:T(8,128)S(1)}, f32[8,16384]{1,0:T(8,128)}, u32[]{:S(2)}) copy-start(f32[8,16384]{1,0:T(8,128)} %get-tuple-element.134) | copy-start | bytes 1572868
  1725.6 90.4 %copy-start.23 = (f32[8,16384]{1,0:T(8,128)S(1)}, f32[8,16384]{1,0:T(8,128)}, u32[]{:S(2)}) copy-start(f32[8,16384]{1,0:T(8,128)} %get-tuple-element.135) | copy-start | bytes 1572868
  1725.6 90.4 %copy-start.113 = (f32[16384]{0:T(1024)S(1)}, f32[16384]{0:T(1024)}, u32[]{:S(2)}) copy-start(f32[16384]{0:T(1024)} %multiply_add_fusion.15) | copy-start | bytes 196612
  1725.6 90.4 %copy-start.123 = (f32[8]{0:T(128)S(1)}, f32[8]{0:T(128)}, u32[]{:S(2)}) copy-start(f32[8]{0:T(128)} %get-tuple-element.39) | copy-start | bytes 100
  1805.9 58.4 %all-to-all-start.7 = ((f32[128,3,1,128]{3,2,1,0:T(1,128)}), f32[128,3,1,128]{3,2,1,0:T(1,128)S(1)}, u32[]{:S(2)}, u32[]{:S(2)}) async-start(f32[128,3,1,128]{3,2,1,0:T(1,128)} %constant_dynamic-update-slice_fusion.384), calls=%async_computation.7 | async-start | bytes 393216 | tf_op jit(solution)/shard_map/all_to_all | solution.py:127
  (157 other events, 2129.5 us)
